TPU v7x, 32 devices: a whole 2x2x4 slice. The times are simulated.
32 devices in a mesh: tm: 2 (over y), space: 16 (over z, x, core).
Axes of the slice: x: 2, y: 2, z: 4, core: 2. Of those that a mesh axis runs over, the one named last changes fastest.
Arguments:
- control: float32 [32, 51200], P(('tm', 'space')), may hold values from -4 to 4
- spectrum: float32 [51200], replicated, may hold values from 0.2 to 2
- perturb: bfloat16 [4, 32, 4, 51200], P('tm', None, None, 'space'), may hold values from -1 to 1
- obs_index: int32 [4, 32768], P('tm', 'space'), may hold values from 0 to 12799
- innovation: float32 [4, 32768], P('tm', 'space'), may hold values from -10 to 10
- obs_sigma: float32 [4, 32768], P('tm', 'space'), may hold values from 0.5 to 2
- qc_class: int32 [4, 32768], P('tm', 'space'), may hold values from 0 to 2
Outputs:
- control_out: float32 [32, 51200], P(('tm', 'space'))
- cost_list: float32 [1], replicated
Inputs may be any that keep to these rules, and one draw needn't show every extreme that they name: `obs_index`: observation o of block o // 2048 observes the cell level * 3200 + point, the point counted within the block's piece of the grid; repeats may occur.
All inputs are finite; a program needn't handle non-finite values.
Results may differ from a plain program's by a relative error of at most 0.0034.
Values may be sent and summed in bfloat16 or wider, within the bound.
A program may use at most 128 MiB of HBM per device.

v0:
```python
import jax
import jax.numpy as jnp
from jax import lax
from jax.sharding import PartitionSpec as P

GX = 320
GY = 160


def lookup_tables(segment_length):
    wave_num = jnp.arange(segment_length, dtype=jnp.float32)[:, None]
    grid_positions = jnp.arange(segment_length, dtype=jnp.float32)[None, :]
    basis = jnp.cos(jnp.pi * (grid_positions + 0.5) * wave_num / segment_length) * jnp.sqrt(
        2.0 / segment_length
    )
    return jnp.where(wave_num == 0, basis * jnp.sqrt(0.5), basis)


def synthesize(control, spectrum, basis_x, basis_y):
    coeffs = (control * spectrum[None, :]).reshape(control.shape[0], GX, GY)
    middle = jnp.einsum("kn,mkl->mnl", basis_x, coeffs, precision=lax.Precision.HIGHEST)
    result = jnp.einsum("mnl,lp->mnp", middle, basis_y, precision=lax.Precision.HIGHEST)
    return result.reshape(control.shape[0], GX * GY)


def analyze(adjoint, spectrum, basis_x, basis_y):
    state_fields = adjoint.reshape(adjoint.shape[0], GX, GY)
    middle = jnp.einsum("kn,mnp->mkp", basis_x, state_fields, precision=lax.Precision.HIGHEST)
    result = jnp.einsum("mkp,lp->mkl", middle, basis_y, precision=lax.Precision.HIGHEST)
    return result.reshape(adjoint.shape[0], GX * GY) * spectrum[None, :]


def per_device(control, spectrum, perturb, obs_index, innovation, obs_sigma, qc_class):
    basis_x = lookup_tables(GX)
    basis_y = lookup_tables(GY)
    slot_count = perturb.shape[0]
    levels = perturb.shape[2]
    piece_len = perturb.shape[3]
    radius = jnp.where(qc_class == 0, 4.0, jnp.where(qc_class == 1, 2.0, 1.0)).astype(jnp.float32)

    def scatter_cells(indices, values):
        return jnp.zeros((levels * piece_len,), jnp.float32).at[indices].add(values)

    member_field = synthesize(control, spectrum, basis_x, basis_y).astype(jnp.bfloat16)
    pieces = lax.all_to_all(member_field, "space", split_axis=1, concat_axis=0, tiled=True)
    selected_entries = perturb
    increment = jnp.einsum(
        "dzab,zb->dab",
        selected_entries,
        lax.all_gather(pieces, "tm", axis=0, tiled=True),
        preferred_element_type=jnp.float32,
    )
    cells_flat = increment.reshape(slot_count, levels * piece_len)
    modelled = jnp.take_along_axis(cells_flat, obs_index, axis=1)
    scaled = (modelled - innovation) / obs_sigma
    scaled_sq = scaled * scaled / (radius * radius)
    obs_part = jnp.sum(0.5 * radius * radius * jnp.log1p(scaled_sq))
    back_part = 0.5 * jnp.sum(control * control)
    obs_grad = scaled / ((1.0 + scaled_sq) * obs_sigma)
    control_update = jax.vmap(scatter_cells)(obs_index, obs_grad).astype(jnp.bfloat16)
    control_update = control_update.reshape(slot_count, levels, piece_len)
    selected_entries = perturb
    summed_rows = lax.psum_scatter(
        jnp.einsum(
            "qiyr,qyr->ir", selected_entries, control_update, preferred_element_type=jnp.float32
        ).astype(jnp.bfloat16),
        "tm",
        scatter_dimension=0,
        tiled=True,
    ).astype(jnp.float32)
    adjoint = lax.all_to_all(
        summed_rows.astype(jnp.bfloat16), "space", split_axis=0, concat_axis=1, tiled=True
    ).astype(summed_rows.dtype)
    gradient = control + analyze(adjoint, spectrum, basis_x, basis_y)
    grad_part = jnp.sum(gradient * gradient)
    obs_cost, back_cost = lax.psum((obs_part, back_part), ("tm", "space"))
    grad_sq = lax.psum(grad_part, ("tm", "space"))
    total_cost = back_cost + obs_cost
    step_size = 0.5 * total_cost / (grad_sq + 1e-06)
    control = control - step_size * gradient
    cost_list = [total_cost]
    return (control, jnp.stack(cost_list))


def solution(mesh):
    in_specs = (
        P(("tm", "space"), None),
        P(),
        P("tm", None, None, "space"),
        P("tm", "space"),
        P("tm", "space"),
        P("tm", "space"),
        P("tm", "space"),
    )
    out_specs = (P(("tm", "space"), None), P())
    return jax.shard_map(
        per_device, mesh=mesh, in_specs=in_specs, out_specs=out_specs, check_vma=False
    )
```

profile of v0, /device:TPU:0, one launch (start us, length us, event | category | flops | bytes accessed | tf_op | source)
XLA Modules:
  0.0 175.1 jit_solution(5619311376740743592)
XLA Ops:
  7.2 2.4 %multiply_reduce_fusion.4 = (f32[]{:T(128)}, f32[51200]{0:T(1024)S(1)}) fusion(f32[1,51200]{1,0:T(1,128)} %param.7, f32[1,51200]{1,0:T(1,128)} %bitcast.56), kind=kLoop, calls=%fused_computation.23 | loop fusion | flops 153599 | bytes 614404 | tf_op jit(solution)/shard_map/reduce_sum | solution.py:58
  9.6 0.1 reshape.98
  9.8 2.6 %convolution_bitcast_fusion.1 = f32[320,160]{0,1:T(8,128)S(1)} fusion(f32[320,160]{1,0:T(8,128)S(1)} %reshape.98, f32[320]{0:T(512)S(1)} %add_multiply_fusion, pred[320]{0:T(512)(128)(4,1)S(1)} %iota_compare_fusion), kind=kOutput, calls=%fused_computation.5 | convolution fusion | flops 197120000 | bytes 411200 | tf_op jit(solution)/shard_map/kn,mkl->mnl/dot_general | solution.py:21
  12.4 1.1 convolution_convert_fusion
  13.5 0.0 copy-start
  13.5 0.1 copy.14
  13.6 0.3 convert_element_type.33
  13.9 0.5 broadcast.94
  14.4 1.2 reduce.13
  15.5 0.8 reshape.139
  16.3 7.4 %all-to-all-start = ((bf16[16,2,1600]{2,1,0:T(2,128)(2,1)}), bf16[16,2,1600]{2,1,0:T(2,128)(2,1)S(1)}, u32[]{:S(2)}, u32[]{:S(2)}) async-start(bf16[16,2,1600]{2,1,0:T(2,128)(2,1)} %reshape.139), calls=%async_computation | async-start | bytes 212992 | tf_op jit(solution)/shard_map/all_to_all | solution.py:45
  23.7 0.0 reduce-scatter.2.cloned.1.call-start
  23.8 0.0 copy-done.3
  23.9 0.0 copy-done.7
  23.9 0.1 multiply_reduce_fusion.5
  24.0 0.0 copy-done.8
  24.0 0.1 and_reduce_fusion
  24.1 7.1 %all-to-all-done = bf16[16,2,1600]{2,1,0:T(2,128)(2,1)S(1)} async-done(((bf16[16,2,1600]{2,1,0:T(2,128)(2,1)}), bf16[16,2,1600]{2,1,0:T(2,128)(2,1)S(1)}, u32[]{:S(2)}, u32[]{:S(2)}) %all-to-all-start) | async-done | bytes 102432 | tf_op jit(solution)/shard_map/all_to_all | solution.py:45
  31.2 0.2 reshape.140
  31.4 5.3 %all-gather = bf16[1,32,3200]{2,1,0:T(8,128)(2,1)S(1)} all-gather(bf16[1,16,3200]{2,1,0:T(8,128)(2,1)S(1)} %copy.16), channel_id=2, replica_groups=mesh['tm'=2,'space'=16] {'tm'}, dimensions={1}, use_global_device_ids=true | all-gather | bytes 307200 | tf_op jit(solution)/shard_map/all_gather | solution.py:50
  36.8 0.9 multiply_reduce_fusion.1
  37.7 0.1 copy.36
  37.7 0.0 copy-start.4
  37.8 0.0 copy-start.5
  37.8 0.0 copy-start.6
  37.8 34.9 %gather_fusion = f32[4096]{0:T(1024)S(1)} fusion(f32[2,12800]{1,0:T(2,128)S(1)} %bitcast.52, s32[4096]{0:T(1024)S(1)} %bitcast.53), kind=kCustom, calls=%fused_computation | custom fusion | bytes 65536 | tf_op jit(solution)/shard_map/jit(take_along_axis)/gather | solution.py:54
  72.7 0.0 copy-done.4
  72.7 0.0 copy-done.5
  72.7 0.0 copy-done.6
  72.7 0.8 fusion.26
  73.5 21.9 %scatter_custom_fusion = f32[25600]{0:T(1024)S(1)} fusion(s32[4096]{0:T(1024)S(1)} %bitcast.61, f32[4096]{0:T(1024)S(1)} %bitcast.62, f32[]{:T(128)} %constant.17.clone.1), kind=kCustom, calls=%fused_computation.39 | custom fusion | flops 4096 | bytes 102404
  95.5 2.2 %multiply_reduce_fusion = bf16[3200,32]{0,1:T(8,128)(2,1)} fusion(f32[3200,2,4]{0,2,1:T(4,128)S(1)} %bitcast_convert_fusion.1, bf16[2,32,4,3200]{3,2,1,0:T(4,128)(2,1)S(1)} %copy-done), kind=kLoop, calls=%fused_computation.2 | loop fusion | flops 2355200 | bytes 1945600 | tf_op jit(solution)/shard_map/qiyr,qyr->ir/dot_general | solution.py:64
  97.7 0.0 reduce-scatter.2.cloned.1.call-update
  97.7 9.2 %reduce-scatter.2.cloned.1.call-done = bf16[16,3200]{1,0:T(8,128)(2,1)} async-done(((bf16[32,3200]{1,0:T(8,128)(2,1)}), bf16[16,3200]{1,0:T(8,128)(2,1)}) %reduce-scatter.2.cloned.1.call-update) | async-done | bytes 102416 | tf_op jit(solution)/shard_map/reduce_scatter | solution.py:63
  106.9 1.5 reduce.14
  108.4 0.8 reshape.141
  109.2 5.7 %all-to-all-start.1 = ((bf16[16,2,1600]{2,1,0:T(2,128)(2,1)}), bf16[16,2,1600]{2,1,0:T(2,128)(2,1)S(1)}, u32[]{:S(2)}, u32[]{:S(2)}) async-start(bf16[16,2,1600]{2,1,0:T(2,128)(2,1)} %reshape.141), calls=%async_computation.2 | async-start | bytes 212992 | tf_op jit(solution)/shard_map/all_to_all | solution.py:71
  116.3 6.2 %all-to-all-done.1 = bf16[16,2,1600]{2,1,0:T(2,128)(2,1)S(1)} async-done(((bf16[16,2,1600]{2,1,0:T(2,128)(2,1)}), bf16[16,2,1600]{2,1,0:T(2,128)(2,1)S(1)}, u32[]{:S(2)}, u32[]{:S(2)}) %all-to-all-start.1) | async-done | bytes 102432 | tf_op jit(solution)/shard_map/all_to_all | solution.py:71
  122.4 0.2 reshape.142
  122.6 0.0 copy-start.1
  122.6 0.6 reduce.5
  123.2 0.2 reshape.103
  123.4 2.3 %convolution_bitcast_fusion = f32[320,160]{0,1:T(8,128)S(1)} fusion(bf16[320,160]{1,0:T(8,128)(2,1)S(1)} %reshape.103, f32[320]{0:T(512)S(1)} %add_multiply_fusion, pred[320]{0:T(512)(128)(4,1)S(1)} %iota_compare_fusion), kind=kOutput, calls=%fused_computation.4 | convolution fusion | flops 197120000 | bytes 308800 | tf_op jit(solution)/shard_map/kn,mnp->mkp/dot_general | solution.py:28
  125.7 1.3 fusion.10
  127.0 0.3 reshape.105
  127.3 1.0 multiply_reduce_fusion.2
  128.4 37.6 %all-reduce = (f32[]{:T(128)}, f32[]{:T(128)}) all-reduce(f32[]{:T(128)S(6)} %add.65, f32[]{:T(128)} %get-tuple-element.6), channel_id=1, replica_groups=mesh['tm'=2,'space'=16] {'tm','space'}, use_global_device_ids=true, to_apply=%region_1.2 | all-reduce | flops 2 | bytes 16 | tf_op jit(solution)/shard_map/psum | solution.py:76
  167.3 0.9 multiply_subtract_fusion
  (26 shorter events, 0.3 us)
Async XLA Ops:
  9.6 14.2 %copy-start.3 = (s32[2,2048]{1,0:T(2,128)S(1)}, s32[2,2048]{1,0:T(2,128)}, u32[]{:S(2)}) copy-start(s32[2,2048]{1,0:T(2,128)} %param.10) | copy-start | bytes 49156
  9.6 14.2 %copy-start.7 = (s32[2]{0:T(128)S(1)}, s32[2]{0:T(128)}, u32[]{:S(2)}) copy-start(s32[2]{0:T(128)} %constant.15) | copy-start | bytes 28
  9.6 14.3 %copy-start.8 = (s32[2]{0:T(128)S(1)}, s32[2]{0:T(128)}, u32[]{:S(2)}) copy-start(s32[2]{0:T(128)} %constant.61) | copy-start | bytes 28
  13.5 23.3 %copy-start = (bf16[2,32,4,3200]{3,2,1,0:T(4,128)(2,1)S(1)}, bf16[2,32,4,3200]{3,2,1,0:T(4,128)(2,1)}, u32[]{:S(2)}) copy-start(bf16[2,32,4,3200]{3,2,1,0:T(4,128)(2,1)} %param.9) | copy-start | bytes 4915204
  16.3 14.9 %all-to-all-start = ((bf16[16,2,1600]{2,1,0:T(2,128)(2,1)}), bf16[16,2,1600]{2,1,0:T(2,128)(2,1)S(1)}, u32[]{:S(2)}, u32[]{:S(2)}) async-start(bf16[16,2,1600]{2,1,0:T(2,128)(2,1)} %reshape.139), calls=%async_computation | async-start | bytes 212992 | tf_op jit(solution)/shard_map/all_to_all | solution.py:45
  23.7 83.2 %reduce-scatter.2.cloned.1.call-start = ((), (), s32[]{:S(2)}) async-start(), calls=%async_computation.3 | async-start | bytes 307200 | tf_op jit(solution)/shard_map/reduce_scatter | solution.py:63
  37.7 35.0 %copy-start.4 = (f32[2,2048]{1,0:T(2,128)S(1)}, f32[2,2048]{1,0:T(2,128)}, u32[]{:S(2)}) copy-start(f32[2,2048]{1,0:T(2,128)} %param.12) | copy-start | bytes 49156
  37.8 35.0 %copy-start.5 = (f32[2,2048]{1,0:T(2,128)S(1)}, f32[2,2048]{1,0:T(2,128)}, u32[]{:S(2)}) copy-start(f32[2,2048]{1,0:T(2,128)} %param.11) | copy-start | bytes 49156
  37.8 35.0 %copy-start.6 = (s32[2,2048]{1,0:T(2,128)S(1)}, s32[2,2048]{1,0:T(2,128)}, u32[]{:S(2)}) copy-start(s32[2,2048]{1,0:T(2,128)} %param.13) | copy-start | bytes 49156
  109.2 18.1 %copy-start.2 = (f32[51200]{0:T(1024)S(1)}, f32[51200]{0:T(1024)}, u32[]{:S(2)}) copy-start(f32[51200]{0:T(1024)} %param.8) | copy-start | bytes 614404
  109.2 13.2 %all-to-all-start.1 = ((bf16[16,2,1600]{2,1,0:T(2,128)(2,1)}), bf16[16,2,1600]{2,1,0:T(2,128)(2,1)S(1)}, u32[]{:S(2)}, u32[]{:S(2)}) async-start(bf16[16,2,1600]{2,1,0:T(2,128)(2,1)} %reshape.141), calls=%async_computation.2 | async-start | bytes 212992 | tf_op jit(solution)/shard_map/all_to_all | solution.py:71
  122.6 4.7 %copy-start.1 = (f32[1,51200]{1,0:T(1,128)S(1)}, f32[1,51200]{1,0:T(1,128)}, u32[]{:S(2)}) copy-start(f32[1,51200]{1,0:T(1,128)} %param.7) | copy-start | bytes 614404
Sparse Core Ops, SparseCore 0:
  97.8 8.9 reduce-scatter.1
where the time goes:
time: 176 us; the launch traced here: 175 us
  blocking collectives  42.9 us (24%)
  local copies, waits for them, and re-layouts  38.5 us (22%)
  other arithmetic  33.7 us (19%)
  waiting for transfers between devices  22.5 us (13%)
  between operations  17 us (10%)
  starting transfers between devices  13.2 us (8%)
  matrix products  7.25 us (4%)
    psum x1, blocking collectives, per_device(): obs_cost, back_cost = lax.psum((obs_part, back_part), ('tm', 'space'))  37.6 us
    gather x3, local copies, waits for them, and re-layouts, per_device(): modelled = jnp.take_along_axis(cells_flat, obs_index, axis=1)  34.9 us
    unnamed x9, other arithmetic  23.4 us
    reduce_scatter x1, waiting for transfers between devices, per_device(): lax.psum_scatter(jnp.einsum('qiyr,qyr->ir', selected_entries, control_upd...  9.17 us
    all_to_all x1, starting transfers between devices, per_device(): lax.all_to_all(member_field, 'space', split_axis=1, concat_axis=0, tiled=...  7.38 us
    all_to_all x1, waiting for transfers between devices, per_device(): lax.all_to_all(member_field, 'space', split_axis=1, concat_axis=0, tiled=...  7.12 us
    all_to_all x1, waiting for transfers between devices, per_device(): lax.all_to_all(summed_rows.astype(jnp.bfloat16), 'space', split_axis=0, c...  6.16 us
    all_to_all x1, starting transfers between devices, per_device(): lax.all_to_all(summed_rows.astype(jnp.bfloat16), 'space', split_axis=0, c...  5.73 us
  transfers between devices with their start and end apart: 3, of which 3 were waited for; matrix products, arithmetic and copies ran while one was open for 0% of the time, Pallas kernels for 0%

commit v1 on v0

--- a/solution.py
+++ b/solution.py
@@ -1,6 +1,12 @@
+import functools
+
 import jax
 import jax.numpy as jnp
+import ml_dtypes
+import numpy as np
 from jax import lax
+from jax.experimental import pallas as pl
+from jax.experimental.pallas import tpu as pltpu
 from jax.sharding import PartitionSpec as P
 
 GX = 320
@@ -82,7 +88,375 @@
     return (control, jnp.stack(cost_list))
 
 
+LANES = 128
+FOLD = 4
+MESH_ID = pl.DeviceIdType.MESH
+F32 = jnp.float32
+BF16 = jnp.bfloat16
+
+
+def basis64(n):
+    k = np.arange(n, dtype=np.float64)[:, None]
+    x = np.arange(n, dtype=np.float64)[None, :]
+    c = np.sqrt(2.0 / n) * np.cos(np.pi * (x + 0.5) * k / n)
+    c[0] *= np.sqrt(0.5)
+    return c.astype(np.float32)
+
+
+def two_parts(c):
+    hi = c.astype(ml_dtypes.bfloat16)
+    lo = (c - hi.astype(np.float32)).astype(ml_dtypes.bfloat16)
+    return np.stack([hi, lo])
+
+
+def folded_bases():
+    cx, cy = basis64(GX), basis64(GY)
+    order = np.arange(GX).reshape(GX // FOLD, FOLD).T.reshape(-1)
+    cxp = cx[order][:, order]
+    return [two_parts(np.ascontiguousarray(a)) for a in (cxp, cxp.T, cy, cy.T)]
+
+
+def split2(x):
+    hi = x.astype(BF16)
+    return hi, (x - hi.astype(F32)).astype(BF16)
+
+
+def split3(x):
+    a = x.astype(BF16).astype(F32)
+    b = (x - a).astype(BF16).astype(F32)
+    return a, b, x - a - b
+
+
+def mm(a, b):
+    return jnp.dot(a, b, preferred_element_type=F32)
+
+
+def dot_right(x, c_ref):
+    hi, lo = split2(x)
+    return mm(hi, c_ref[0]) + (mm(lo, c_ref[0]) + mm(hi, c_ref[1]))
+
+
+def dot_left(c_ref, x):
+    hi, lo = split2(x)
+    return mm(c_ref[0], hi) + (mm(c_ref[0], lo) + mm(c_ref[1], hi))
+
+
+def unfold(wide):
+    return jnp.concatenate([wide[:, r * GY : (r + 1) * GY] for r in range(FOLD)], axis=0)
+
+
+def fold(tall):
+    q = GX // FOLD
+    return jnp.concatenate([tall[r * q : (r + 1) * q] for r in range(FOLD)], axis=1)
+
+
+def step_kernel(
+    nt, ns, control, spectrum, perturb_hbm, index, innov, sigma, qc, cxp, cxpt, cy, cyt,
+    out, cost_out,
+    perturb, flat, send_f, recv_f, inc, table, hi_hot, lo_hot, upd, adj_row, send_a, recv_a,
+    part, parts, grad, p_sem, sf_sem, rf_sem, sa_sem, ra_sem, sp_sem, rp_sem,
+):
+    n = nt * ns
+    my_t, my_s = lax.axis_index("tm"), lax.axis_index("space")
+    me = my_t * ns + my_s
+    slots, members, levels, piece = perturb.shape
+    rows = piece // LANES
+    pad_rows = send_f.shape[1]
+    q, width = GX // FOLD, FOLD * GY
+    tiles = width // LANES
+    obs = index.shape[1]
+
+    def peer_of(d):
+        peer = (me + d) % n
+        return peer, (peer // ns, peer % ns)
+
+    load_p = pltpu.make_async_copy(perturb_hbm, perturb, p_sem)
+    load_p.start()
+
+    barrier = pltpu.get_barrier_semaphore()
+
+    def greet(d, c):
+        pl.semaphore_signal(barrier, inc=1, device_id=peer_of(d)[1], device_id_type=MESH_ID)
+        return c
+
+    lax.fori_loop(1, n, greet, 0)
+
+    def wide_of(ref):
+        return jnp.concatenate(
+            [ref[pl.ds(a, q, stride=tiles), :] for a in range(tiles)], axis=1
+        )
+
+    def flat_from(wide):
+        for a in range(tiles):
+            flat[pl.ds(a, q, stride=tiles), :] = wide[:, a * LANES : (a + 1) * LANES]
+
+    ctl = wide_of(control)
+    spec = wide_of(spectrum)
+    mid = dot_right(unfold(ctl * spec), cy)
+    flat_from(fold(dot_left(cxpt, mid)))
+    flat[q * tiles :, :] = jnp.zeros((flat.shape[0] - q * tiles, LANES), F32)
+    for s in range(ns):
+        send_f[s] = flat[s * rows : s * rows + pad_rows, :].astype(BF16)
+    back = 0.5 * jnp.sum(ctl * ctl, axis=0, keepdims=True)
+    back = sum(back[:, a * LANES : (a + 1) * LANES] for a in range(tiles))
+
+    pl.semaphore_wait(barrier, n - 1)
+
+    def f_copy(d):
+        peer, dev = peer_of(d)
+        return pltpu.make_async_remote_copy(
+            send_f.at[peer % ns], recv_f.at[me], sf_sem.at[peer], rf_sem.at[me],
+            device_id=dev, device_id_type=MESH_ID,
+        )
+
+    def start_f(d, c):
+        f_copy(d).start()
+        return c
+
+    lax.fori_loop(1, n, start_f, 0)
+    recv_f[me] = send_f[my_s]
+
+    table[...] = jnp.zeros(table.shape, F32)
+    hi_rows = table.shape[1]
+    his, los = [], []
+    for t in range(slots):
+        ix = index[t : t + 1, :]
+        level, point = ix // piece, ix % piece
+        hi, lo = (point // LANES) * levels + level, point % LANES
+        his.append(hi)
+        los.append(lo)
+        hi_hot[t] = jnp.where(
+            lax.broadcasted_iota(jnp.int32, (hi_rows, obs), 0) == hi, 1.0, 0.0
+        ).astype(BF16)
+        lo_hot[t] = jnp.where(
+            lax.broadcasted_iota(jnp.int32, (LANES, obs), 0) == lo, 1.0, 0.0
+        ).astype(BF16)
+    inc[...] = jnp.zeros(inc.shape, F32)
+    load_p.wait()
+
+    def wait_f(d, c):
+        src = (me + n - d) % n
+        pltpu.make_async_remote_copy(
+            send_f.at[0], recv_f.at[src], sf_sem.at[src], rf_sem.at[src],
+            device_id=(src // ns, src % ns), device_id_type=MESH_ID,
+        ).wait_recv()
+        return c
+
+    lax.fori_loop(1, n, wait_f, 0)
+
+    group = 8
+
+    def add_group(g, c):
+        fs = [recv_f[g * group + i].astype(F32) for i in range(group)]
+        for j in range(rows):
+            at = pl.ds(j * LANES, LANES)
+            fb = [jnp.broadcast_to(f[j : j + 1, :], (levels, LANES)) for f in fs]
+            for t in range(slots):
+                total = inc[t, :, at]
+                for i in range(group):
+                    total = total + perturb[t, g * group + i, :, at].astype(F32) * fb[i]
+                inc[t, :, at] = total
+        return c
+
+    lax.fori_loop(0, members // group, add_group, 0)
+
+    cost_row = back
+    for t in range(slots):
+        for j in range(rows):
+            table[t, j * levels : (j + 1) * levels, :] = inc[t, :, j * LANES : (j + 1) * LANES]
+        three = jnp.concatenate(split3(table[t]), axis=1).T.astype(BF16)
+        picked = mm(three, hi_hot[t])
+        picked = picked[:LANES] + picked[LANES : 2 * LANES] + picked[2 * LANES :]
+        at_lo = lax.broadcasted_iota(jnp.int32, (LANES, obs), 0) == los[t]
+        model = jnp.sum(jnp.where(at_lo, picked, 0.0), axis=0, keepdims=True)
+        sg = sigma[t : t + 1, :]
+        qct = qc[t : t + 1, :]
+        rad = jnp.where(qct == 0, 4.0, jnp.where(qct == 1, 2.0, 1.0)).astype(F32)
+        scaled = (model - innov[t : t + 1, :]) / sg
+        sq = scaled * scaled / (rad * rad)
+        cost = 0.5 * rad * rad * jnp.log1p(sq)
+        cost_row = cost_row + sum(cost[:, a : a + LANES] for a in range(0, obs, LANES))
+        g = scaled / ((1.0 + sq) * sg)
+        at_hi = lax.broadcasted_iota(jnp.int32, (hi_rows, obs), 0) == his[t]
+        terms = jnp.concatenate(
+            [jnp.where(at_hi, p, 0.0).astype(BF16) for p in split3(g)], axis=0
+        )
+        u = lax.dot_general(
+            terms, lo_hot[t], (((1,), (1,)), ((), ())), preferred_element_type=F32
+        )
+        u = u[:hi_rows] + u[hi_rows : 2 * hi_rows] + u[2 * hi_rows :]
+        table[t] = u.astype(BF16).astype(F32)
+        for j in range(rows):
+            upd[t, :, j * LANES : (j + 1) * LANES] = table[t, j * levels : (j + 1) * levels, :]
+
+    def a_copy(d):
+        peer, dev = peer_of(d)
+        return pltpu.make_async_remote_copy(
+            send_a.at[peer], recv_a.at[me], sa_sem.at[peer], ra_sem.at[me],
+            device_id=dev, device_id_type=MESH_ID,
+        )
+
+    adj_row[...] = jnp.zeros(adj_row.shape, F32)
+
+    def one_member(d):
+        m = (me + d) % n
+        for j in range(rows):
+            at = pl.ds(j * LANES, LANES)
+            z = sum(perturb[t, m, :, at].astype(F32) * upd[t, :, at] for t in range(slots))
+            adj_row[j : j + 1, :] = jnp.sum(z, axis=0, keepdims=True)
+        send_a[m] = adj_row[...].astype(BF16)
+
+    one_member(1)
+
+    def next_member(d, c):
+        one_member(d)
+        a_copy(d - 1).start()
+        return c
+
+    lax.fori_loop(2, n + 1, next_member, 0)
+    recv_a[me] = send_a[me]
+
+    def wait_a(d, c):
+        src = (me + n - d) % n
+        pltpu.make_async_remote_copy(
+            send_a.at[0], recv_a.at[src], sa_sem.at[src], ra_sem.at[src],
+            device_id=(src // ns, src % ns), device_id_type=MESH_ID,
+        ).wait_recv()
+        return c
+
+    lax.fori_loop(1, n, wait_a, 0)
+
+    for s in range(ns):
+        whole = sum(recv_a[t * ns + s].astype(F32) for t in range(nt))
+        flat[s * rows : (s + 1) * rows, :] = whole[:rows]
+    mid = dot_left(cxp, unfold(wide_of(flat)))
+    gr = ctl + spec * fold(dot_right(mid, cyt))
+    grad[...] = gr
+    sq = jnp.sum(gr * gr, axis=0, keepdims=True)
+    sq = sum(sq[:, a * LANES : (a + 1) * LANES] for a in range(tiles))
+    part[0:1, :] = cost_row
+    part[1:2, :] = sq
+
+    def s_copy(d):
+        peer, dev = peer_of(d)
+        return pltpu.make_async_remote_copy(
+            part, parts.at[me], sp_sem.at[peer], rp_sem.at[me],
+            device_id=dev, device_id_type=MESH_ID,
+        )
+
+    def start_s(d, c):
+        s_copy(d).start()
+        return c
+
+    lax.fori_loop(1, n, start_s, 0)
+    parts[me] = part[...]
+
+    def drain(d, c):
+        f_copy(d).wait_send()
+        a_copy(d).wait_send()
+        return c
+
+    lax.fori_loop(1, n, drain, 0)
+
+    def wait_s(d, c):
+        src = (me + n - d) % n
+        pltpu.make_async_remote_copy(
+            part, parts.at[src], sp_sem.at[src], rp_sem.at[src],
+            device_id=(src // ns, src % ns), device_id_type=MESH_ID,
+        ).wait_recv()
+        return c
+
+    lax.fori_loop(1, n, wait_s, 0)
+    sums = jnp.sum(jnp.sum(parts[...], axis=0), axis=1, keepdims=True)
+    total_cost, grad_sq = sums[0:1, :], sums[1:2, :]
+    step = 0.5 * total_cost / (grad_sq + 1e-06)
+    new = ctl - step * grad[...]
+    for a in range(tiles):
+        out[pl.ds(a, q, stride=tiles), :] = new[:, a * LANES : (a + 1) * LANES]
+    cost_out[...] = jnp.broadcast_to(total_cost, cost_out.shape)
+
+    def drain_s(d, c):
+        s_copy(d).wait_send()
+        return c
+
+    lax.fori_loop(1, n, drain_s, 0)
+
+
+def fused_device(nt, ns, control, spectrum, perturb, obs_index, innovation, obs_sigma, qc_class):
+    n = nt * ns
+    slots, members, levels, piece = perturb.shape
+    grid_rows = GX * GY // LANES
+    rows = piece // LANES
+    pad_rows = -(-rows // 16) * 16
+    hi_rows = -(-rows * levels // 16) * 16
+    obs = obs_index.shape[1]
+    vm = pl.BlockSpec(memory_space=pltpu.VMEM)
+    dma = pltpu.SemaphoreType.DMA
+    bases = [jnp.asarray(b) for b in folded_bases()]
+    out, cost = pl.pallas_call(
+        functools.partial(step_kernel, nt, ns),
+        out_shape=(
+            jax.ShapeDtypeStruct((grid_rows, LANES), F32),
+            jax.ShapeDtypeStruct((1, LANES), F32),
+        ),
+        in_specs=[vm, vm, pl.BlockSpec(memory_space=pl.ANY)] + [vm] * 8,
+        out_specs=(vm, vm),
+        scratch_shapes=[
+            pltpu.VMEM(perturb.shape, BF16),
+            pltpu.VMEM((grid_rows + 16, LANES), F32),
+            pltpu.VMEM((ns, pad_rows, LANES), BF16),
+            pltpu.VMEM((n, pad_rows, LANES), BF16),
+            pltpu.VMEM((slots, levels, piece), F32),
+            pltpu.VMEM((slots, hi_rows, LANES), F32),
+            pltpu.VMEM((slots, hi_rows, obs), BF16),
+            pltpu.VMEM((slots, LANES, obs), BF16),
+            pltpu.VMEM((slots, levels, piece), F32),
+            pltpu.VMEM((pad_rows, LANES), F32),
+            pltpu.VMEM((n, pad_rows, LANES), BF16),
+            pltpu.VMEM((n, pad_rows, LANES), BF16),
+            pltpu.VMEM((2, LANES), F32),
+            pltpu.VMEM((n, 2, LANES), F32),
+            pltpu.VMEM((GX // FOLD, FOLD * GY), F32),
+            dma, dma((n,)), dma((n,)), dma((n,)), dma((n,)), dma((n,)), dma((n,)),
+        ],
+        compiler_params=pltpu.CompilerParams(
+            collective_id=0, has_side_effects=True, vmem_limit_bytes=48 << 20
+        ),
+        name="envar_step",
+    )(
+        control.reshape(grid_rows, LANES), spectrum.reshape(grid_rows, LANES), perturb,
+        obs_index, innovation, obs_sigma, qc_class, *bases,
+    )
+    return out.reshape(control.shape), cost[0, :1]
+
+
+def fused_fits(nt, ns, control, perturb, innovation):
+    n = nt * ns
+    piece = GX * GY // ns
+    return (
+        control.shape[0] == n
+        and piece % LANES == 0
+        and (FOLD * GY) % LANES == 0
+        and (GX // FOLD) % 8 == 0
+        and n % 8 == 0
+        and (innovation.shape[1] // ns) % LANES == 0
+    )
+
+
 def solution(mesh):
+    nt, ns = mesh.shape["tm"], mesh.shape["space"]
+
+    def whole(control, spectrum, perturb, obs_index, innovation, obs_sigma, qc_class):
+        fits = fused_fits(nt, ns, control, perturb, innovation)
+        body = functools.partial(fused_device, nt, ns) if fits else per_device
+        return on_mesh(mesh, body)(
+            control, spectrum, perturb, obs_index, innovation, obs_sigma, qc_class
+        )
+
+    return whole
+
+
+def on_mesh(mesh, body):
     in_specs = (
         P(("tm", "space"), None),
         P(),
@@ -94,5 +468,5 @@
     )
     out_specs = (P(("tm", "space"), None), P())
     return jax.shard_map(
-        per_device, mesh=mesh, in_specs=in_specs, out_specs=out_specs, check_vma=False
-    )
+        body, mesh=mesh, in_specs=in_specs, out_specs=out_specs, check_vma=False
+    )

time: 176 us -> 46.9 us (0.27)
  blocking collectives: 42.9 us -> 0 us
  Pallas kernels: 0 us -> 33.8 us
  other arithmetic: 33.7 us -> 0 us
  local copies, waits for them, and re-layouts: 38.5 us -> 10.7 us
  waiting for transfers between devices: 22.5 us -> 0 us
  between operations: 17 us -> 1.82 us
  starting transfers between devices: 13.2 us -> 0 us
  matrix products: 7.25 us -> 0 us
    psum x1 -> x0, blocking collectives: 37.6 us -> none  [per_device(): obs_cost, back_cost = lax.psum((obs_part, back_part), ('tm', 'space'))]
    gather x3 -> x0, local copies, waits for them, and re-layouts: 34.9 us -> none  [per_device(): modelled = jnp.take_along_axis(cells_flat, obs_index, axis=1)]
    pallas_call x0 -> x1, Pallas kernels: none -> 33.8 us  [fused_device(): pl.pallas_call(functools.partial(step_kernel, nt, ns), out_shape=(jax.Sha...]
    unnamed x9 -> x0, other arithmetic: 23.4 us -> none
    all_to_all x2 -> x0, waiting for transfers between devices: 13.3 us -> none  [the longest x1 7.12 us: per_device(): lax.all_to_all(member_field, 'space', split_axis=1, concat_axis=0, tiled=...]
    all_to_all x2 -> x0, starting transfers between devices: 13.1 us -> none  [the longest x1 7.38 us: per_device(): lax.all_to_all(member_field, 'space', split_axis=1, concat_axis=0, tiled=...]
    reduce_scatter x1 -> x0, waiting for transfers between devices: 9.17 us -> none  [per_device(): lax.psum_scatter(jnp.einsum('qiyr,qyr->ir', selected_entries, control_upd...]
    unnamed x27 -> x23, local copies, waits for them, and re-layouts: 2.56 us -> 10.7 us
  transfers between devices with their start and end apart: 3 -> 0, of which waited for: 3 -> 0; matrix products, arithmetic and copies ran while one was open for 0% -> 0% of each run, Pallas kernels for 0% -> 0%
where the time goes in v1:
time: 46.9 us; the launch traced here: 46.4 us
  Pallas kernels  33.8 us (72%)
  local copies, waits for them, and re-layouts  10.7 us (23%)
  between operations  1.82 us (4%)
    pallas_call x1, Pallas kernels, fused_device(): pl.pallas_call(functools.partial(step_kernel, nt, ns), out_shape=(jax.Sha...  33.8 us
    unnamed x23, local copies, waits for them, and re-layouts  10.7 us

profile of v1, /device:TPU:0, one launch (start us, length us, event | category | flops | bytes accessed | tf_op | source)
XLA Modules:
  0.0 46.4 jit_solution(4701549744625425111)
XLA Ops:
  0.6 0.0 copy-start
  0.6 1.4 %copy-done = bf16[2,32,4,3200]{3,2,1,0:T(4,128)(2,1)S(1)} copy-done((bf16[2,32,4,3200]{3,2,1,0:T(4,128)(2,1)S(1)}, bf16[2,32,4,3200]{3,2,1,0:T(4,128)(2,1)}, u32[]{:S(2)}) %copy-start) | copy-done | bytes 1638424
  2.1 0.0 copy-start.1
  2.1 1.0 %copy-done.1 = bf16[2,320,320]{2,1,0:T(8,128)(2,1)S(1)} copy-done((bf16[2,320,320]{2,1,0:T(8,128)(2,1)S(1)}, bf16[2,320,320]{2,1,0:T(8,128)(2,1)}, u32[]{:S(2)}) %copy-start.1) | copy-done | bytes 409624
  3.1 0.0 copy-start.2
  3.1 1.0 %copy-done.2 = bf16[2,320,320]{2,1,0:T(8,128)(2,1)S(1)} copy-done((bf16[2,320,320]{2,1,0:T(8,128)(2,1)S(1)}, bf16[2,320,320]{2,1,0:T(8,128)(2,1)}, u32[]{:S(2)}) %copy-start.2) | copy-done | bytes 409624
  4.1 0.0 copy-start.3
  4.1 0.9 %copy-done.3 = f32[1,51200]{1,0:T(1,128)S(1)} copy-done((f32[1,51200]{1,0:T(1,128)S(1)}, f32[1,51200]{1,0:T(1,128)}, u32[]{:S(2)}) %copy-start.3) | copy-done | bytes 204824
  5.1 0.0 copy-start.4
  5.1 0.9 %copy-done.4 = f32[51200]{0:T(1024)S(1)} copy-done((f32[51200]{0:T(1024)S(1)}, f32[51200]{0:T(1024)}, u32[]{:S(2)}) %copy-start.4) | copy-done | bytes 204824
  6.0 0.0 copy-start.5
  6.0 0.9 %copy-done.5 = bf16[2,160,160]{2,1,0:T(8,128)(2,1)S(1)} copy-done((bf16[2,160,160]{2,1,0:T(8,128)(2,1)S(1)}, bf16[2,160,160]{2,1,0:T(8,128)(2,1)}, u32[]{:S(2)}) %copy-start.5) | copy-done | bytes 102424
  6.9 0.0 copy-start.6
  6.9 0.9 %copy-done.6 = bf16[2,160,160]{2,1,0:T(8,128)(2,1)S(1)} copy-done((bf16[2,160,160]{2,1,0:T(8,128)(2,1)S(1)}, bf16[2,160,160]{2,1,0:T(8,128)(2,1)}, u32[]{:S(2)}) %copy-start.6) | copy-done | bytes 102424
  7.8 0.0 copy-start.7
  7.8 0.7 %copy-done.7 = s32[2,2048]{1,0:T(2,128)S(1)} copy-done((s32[2,2048]{1,0:T(2,128)S(1)}, s32[2,2048]{1,0:T(2,128)}, u32[]{:S(2)}) %copy-start.7) | copy-done | bytes 16408
  8.5 0.0 copy-start.8
  8.5 0.7 %copy-done.8 = f32[2,2048]{1,0:T(2,128)S(1)} copy-done((f32[2,2048]{1,0:T(2,128)S(1)}, f32[2,2048]{1,0:T(2,128)}, u32[]{:S(2)}) %copy-start.8) | copy-done | bytes 16408
  9.3 0.0 copy-start.9
  9.3 0.7 %copy-done.9 = f32[2,2048]{1,0:T(2,128)S(1)} copy-done((f32[2,2048]{1,0:T(2,128)S(1)}, f32[2,2048]{1,0:T(2,128)}, u32[]{:S(2)}) %copy-start.9) | copy-done | bytes 16408
  10.0 0.0 copy-start.10
  10.0 0.7 %copy-done.10 = s32[2,2048]{1,0:T(2,128)S(1)} copy-done((s32[2,2048]{1,0:T(2,128)S(1)}, s32[2,2048]{1,0:T(2,128)}, u32[]{:S(2)}) %copy-start.10) | copy-done | bytes 16408
  10.7 33.8 %envar_step.1 = (f32[400,128]{1,0:T(8,128)S(1)}, f32[1,128]{1,0:T(1,128)S(1)}) custom-call(f32[400,128]{1,0:T(8,128)S(1)} %bitcast.6, f32[400,128]{1,0:T(8,128)S(1)} %bitcast.7, bf16[2,32,4,3200]{3,2,1,0:T(4,128)(2,1)S(1)} %copy-done, s32[2,2048]{1,0:T(2,128)S(1)} %copy-done.7, f32[2,2048]{1,0:T(2,128)S(1)} %copy-done.8, f32[2,2048]{1,0:T(2,128)S(1)} %copy-done.9, ...), custom_call_target="tpu_custom_call" | custom-call | tf_op jit(solution)/shard_map/envar_step/pallas_call | solution.py:396
  44.5 0.7 %copy.15 = f32[1,51200]{1,0:T(1,128)} copy(f32[1,51200]{1,0:T(1,128)S(1)} %bitcast.5) | data formatting | bytes 409600
Async XLA Ops:
  0.6 1.4 %copy-start = (bf16[2,32,4,3200]{3,2,1,0:T(4,128)(2,1)S(1)}, bf16[2,32,4,3200]{3,2,1,0:T(4,128)(2,1)}, u32[]{:S(2)}) copy-start(bf16[2,32,4,3200]{3,2,1,0:T(4,128)(2,1)} %perturb_hbm.1) | copy-start | bytes 4915204
  2.1 1.0 %copy-start.1 = (bf16[2,320,320]{2,1,0:T(8,128)(2,1)S(1)}, bf16[2,320,320]{2,1,0:T(8,128)(2,1)}, u32[]{:S(2)}) copy-start(bf16[2,320,320]{2,1,0:T(8,128)(2,1)} %constant.9.clone.cxpt) | copy-start | bytes 1228804
  3.1 1.0 %copy-start.2 = (bf16[2,320,320]{2,1,0:T(8,128)(2,1)S(1)}, bf16[2,320,320]{2,1,0:T(8,128)(2,1)}, u32[]{:S(2)}) copy-start(bf16[2,320,320]{2,1,0:T(8,128)(2,1)} %constant.8.clone.cxp) | copy-start | bytes 1228804
  4.1 0.9 %copy-start.3 = (f32[1,51200]{1,0:T(1,128)S(1)}, f32[1,51200]{1,0:T(1,128)}, u32[]{:S(2)}) copy-start(f32[1,51200]{1,0:T(1,128)} %param.11) | copy-start | bytes 614404
  5.1 0.9 %copy-start.4 = (f32[51200]{0:T(1024)S(1)}, f32[51200]{0:T(1024)}, u32[]{:S(2)}) copy-start(f32[51200]{0:T(1024)} %param.12) | copy-start | bytes 614404
  6.0 0.9 %copy-start.5 = (bf16[2,160,160]{2,1,0:T(8,128)(2,1)S(1)}, bf16[2,160,160]{2,1,0:T(8,128)(2,1)}, u32[]{:S(2)}) copy-start(bf16[2,160,160]{2,1,0:T(8,128)(2,1)} %constant.11.clone.cyt) | copy-start | bytes 307204
  6.9 0.9 %copy-start.6 = (bf16[2,160,160]{2,1,0:T(8,128)(2,1)S(1)}, bf16[2,160,160]{2,1,0:T(8,128)(2,1)}, u32[]{:S(2)}) copy-start(bf16[2,160,160]{2,1,0:T(8,128)(2,1)} %constant.10.clone.cy) | copy-start | bytes 307204
  7.8 0.7 %copy-start.7 = (s32[2,2048]{1,0:T(2,128)S(1)}, s32[2,2048]{1,0:T(2,128)}, u32[]{:S(2)}) copy-start(s32[2,2048]{1,0:T(2,128)} %index.1) | copy-start | bytes 49156
  8.5 0.7 %copy-start.8 = (f32[2,2048]{1,0:T(2,128)S(1)}, f32[2,2048]{1,0:T(2,128)}, u32[]{:S(2)}) copy-start(f32[2,2048]{1,0:T(2,128)} %innov.1) | copy-start | bytes 49156
  9.3 0.7 %copy-start.9 = (f32[2,2048]{1,0:T(2,128)S(1)}, f32[2,2048]{1,0:T(2,128)}, u32[]{:S(2)}) copy-start(f32[2,2048]{1,0:T(2,128)} %sigma.1) | copy-start | bytes 49156
  10.0 0.7 %copy-start.10 = (s32[2,2048]{1,0:T(2,128)S(1)}, s32[2,2048]{1,0:T(2,128)}, u32[]{:S(2)}) copy-start(s32[2,2048]{1,0:T(2,128)} %qc.1) | copy-start | bytes 49156

commit v2 on v1

--- a/solution.py
+++ b/solution.py
@@ -151,11 +151,15 @@
 
 
 def step_kernel(
-    nt, ns, control, spectrum, perturb_hbm, index, innov, sigma, qc, cxp, cxpt, cy, cyt,
-    out, cost_out,
-    perturb, flat, send_f, recv_f, inc, table, hi_hot, lo_hot, upd, adj_row, send_a, recv_a,
-    part, parts, grad, p_sem, sf_sem, rf_sem, sa_sem, ra_sem, sp_sem, rp_sem,
+    nt, ns, n_in, *refs
 ):
+    sources, (out, cost_out), held = refs[:n_in], refs[n_in : n_in + 2], refs[n_in + 2 :]
+    landed, in_sem, held = held[:n_in], held[n_in], held[n_in + 1 :]
+    control, spectrum, cy, cxpt, index, perturb, innov, sigma, qc, cxp, cyt = landed
+    (
+    flat, send_f, recv_f, inc, table, hi_hot, lo_hot, upd, adj_row, send_a, recv_a,
+    part, parts, grad, sf_sem, rf_sem, sa_sem, ra_sem, sp_sem, rp_sem,
+    ) = held
     n = nt * ns
     my_t, my_s = lax.axis_index("tm"), lax.axis_index("space")
     me = my_t * ns + my_s
@@ -170,8 +174,12 @@
         peer = (me + d) % n
         return peer, (peer // ns, peer % ns)
 
-    load_p = pltpu.make_async_copy(perturb_hbm, perturb, p_sem)
-    load_p.start()
+    loads = [
+        pltpu.make_async_copy(src, dst, in_sem.at[i])
+        for i, (src, dst) in enumerate(zip(sources, landed))
+    ]
+    for load in loads:
+        load.start()
 
     barrier = pltpu.get_barrier_semaphore()
 
@@ -190,6 +198,8 @@
         for a in range(tiles):
             flat[pl.ds(a, q, stride=tiles), :] = wide[:, a * LANES : (a + 1) * LANES]
 
+    for load in loads[:4]:
+        load.wait()
     ctl = wide_of(control)
     spec = wide_of(spectrum)
     mid = dot_right(unfold(ctl * spec), cy)
@@ -216,6 +226,7 @@
     lax.fori_loop(1, n, start_f, 0)
     recv_f[me] = send_f[my_s]
 
+    loads[4].wait()
     table[...] = jnp.zeros(table.shape, F32)
     hi_rows = table.shape[1]
     his, los = [], []
@@ -232,7 +243,8 @@
             lax.broadcasted_iota(jnp.int32, (LANES, obs), 0) == lo, 1.0, 0.0
         ).astype(BF16)
     inc[...] = jnp.zeros(inc.shape, F32)
-    load_p.wait()
+    for load in loads[5:]:
+        load.wait()
 
     def wait_f(d, c):
         src = (me + n - d) % n
@@ -392,17 +404,22 @@
     obs = obs_index.shape[1]
     vm = pl.BlockSpec(memory_space=pltpu.VMEM)
     dma = pltpu.SemaphoreType.DMA
-    bases = [jnp.asarray(b) for b in folded_bases()]
+    cxp, cxpt, cy, cyt = [jnp.asarray(b) for b in folded_bases()]
+    sources = [
+        control.reshape(grid_rows, LANES), spectrum.reshape(grid_rows, LANES), cy, cxpt,
+        obs_index, perturb, innovation, obs_sigma, qc_class, cxp, cyt,
+    ]
     out, cost = pl.pallas_call(
-        functools.partial(step_kernel, nt, ns),
+        functools.partial(step_kernel, nt, ns, len(sources)),
         out_shape=(
             jax.ShapeDtypeStruct((grid_rows, LANES), F32),
             jax.ShapeDtypeStruct((1, LANES), F32),
         ),
-        in_specs=[vm, vm, pl.BlockSpec(memory_space=pl.ANY)] + [vm] * 8,
+        in_specs=[pl.BlockSpec(memory_space=pltpu.HBM)] * len(sources),
         out_specs=(vm, vm),
         scratch_shapes=[
-            pltpu.VMEM(perturb.shape, BF16),
+            *[pltpu.VMEM(a.shape, a.dtype) for a in sources],
+            dma((len(sources),)),
             pltpu.VMEM((grid_rows + 16, LANES), F32),
             pltpu.VMEM((ns, pad_rows, LANES), BF16),
             pltpu.VMEM((n, pad_rows, LANES), BF16),
@@ -417,16 +434,13 @@
             pltpu.VMEM((2, LANES), F32),
             pltpu.VMEM((n, 2, LANES), F32),
             pltpu.VMEM((GX // FOLD, FOLD * GY), F32),
-            dma, dma((n,)), dma((n,)), dma((n,)), dma((n,)), dma((n,)), dma((n,)),
+            dma((n,)), dma((n,)), dma((n,)), dma((n,)), dma((n,)), dma((n,)),
         ],
         compiler_params=pltpu.CompilerParams(
-            collective_id=0, has_side_effects=True, vmem_limit_bytes=48 << 20
+            collective_id=0, has_side_effects=True, vmem_limit_bytes=67043328
         ),
         name="envar_step",
-    )(
-        control.reshape(grid_rows, LANES), spectrum.reshape(grid_rows, LANES), perturb,
-        obs_index, innovation, obs_sigma, qc_class, *bases,
-    )
+    )(*sources)
     return out.reshape(control.shape), cost[0, :1]
 
 

time: 46.9 us -> 38.6 us (0.82)
  local copies, waits for them, and re-layouts: 10.7 us -> 1.62 us
  Pallas kernels: 33.8 us -> 34.5 us
  between operations: 1.82 us -> 2.33 us
    unnamed x23 -> x1, local copies, waits for them, and re-layouts: 10.7 us -> 1.62 us
    pallas_call x1, Pallas kernels: 33.8 us -> 34.5 us  [fused_device(): pl.pallas_call(functools.partial(step_kernel, nt, ns, len(sources)), out_...]
where the time goes in v2:
time: 38.6 us; the launch traced here: 38.4 us
  Pallas kernels  34.5 us (89%)
  between operations  2.33 us (6%)
  local copies, waits for them, and re-layouts  1.62 us (4%)
    pallas_call x1, Pallas kernels, fused_device(): pl.pallas_call(functools.partial(step_kernel, nt, ns, len(sources)), out_...  34.5 us
    unnamed x1, local copies, waits for them, and re-layouts  1.62 us

profile of v2, /device:TPU:0, one launch (start us, length us, event | category | flops | bytes accessed | tf_op | source)
XLA Modules:
  0.0 38.4 jit_solution(14356650702876519160)
XLA Ops:
  0.6 34.5 %envar_step.1 = (f32[400,128]{1,0:T(8,128)}, f32[1,128]{1,0:T(1,128)}) custom-call(f32[400,128]{1,0:T(8,128)} %bitcast.6, f32[400,128]{1,0:T(8,128)} %bitcast.7, bf16[2,160,160]{2,1,0:T(8,128)(2,1)} %constant.10.clone.refs_2_, bf16[2,320,320]{2,1,0:T(8,128)(2,1)} %constant.9.clone.refs_3_, s32[2,2048]{1,0:T(2,128)} %refs_4_.1, ...), custom_call_target="tpu_custom_call" | custom-call | tf_op jit(solution)/shard_map/envar_step/pallas_call | solution.py:412
  35.1 1.6 %copy.15 = f32[1,51200]{1,0:T(1,128)} copy(f32[1,51200]{1,0:T(1,128)} %bitcast.5) | data formatting | bytes 409600

commit v3 on v2

--- a/solution.py
+++ b/solution.py
@@ -157,8 +157,8 @@
     landed, in_sem, held = held[:n_in], held[n_in], held[n_in + 1 :]
     control, spectrum, cy, cxpt, index, perturb, innov, sigma, qc, cxp, cyt = landed
     (
-    flat, send_f, recv_f, inc, table, hi_hot, lo_hot, upd, adj_row, send_a, recv_a,
-    part, parts, grad, sf_sem, rf_sem, sa_sem, ra_sem, sp_sem, rp_sem,
+    flat, send_f, recv_f, inc, table, hi_hot, lo_hot, upd, adj_row, send_y, mid_a,
+    send_a, recv_a, part, parts, grad, sf_sem, rf_sem, sr_sem, sy_sem, ry_sem, sa_sem, ra_sem, sp_sem, rp_sem,
     ) = held
     n = nt * ns
     my_t, my_s = lax.axis_index("tm"), lax.axis_index("space")
@@ -171,8 +171,8 @@
     obs = index.shape[1]
 
     def peer_of(d):
-        peer = (me + d) % n
-        return peer, (peer // ns, peer % ns)
+        peer = lax.rem(me + d, n)
+        return peer, (lax.div(peer, ns), lax.rem(peer, ns))
 
     loads = [
         pltpu.make_async_copy(src, dst, in_sem.at[i])
@@ -212,18 +212,29 @@
 
     pl.semaphore_wait(barrier, n - 1)
 
+    other = (nt - 1 - my_t, my_s)
+
+    def ahead(d):
+        return lax.rem(my_s + d, ns)
+
     def f_copy(d):
-        peer, dev = peer_of(d)
         return pltpu.make_async_remote_copy(
-            send_f.at[peer % ns], recv_f.at[me], sf_sem.at[peer], rf_sem.at[me],
-            device_id=dev, device_id_type=MESH_ID,
+            send_f.at[ahead(d)], recv_f.at[me], sf_sem.at[ahead(d)], rf_sem.at[me],
+            device_id=(my_t, ahead(d)), device_id_type=MESH_ID,
+        )
+
+    def relay(s):
+        slot = my_t * ns + s
+        return pltpu.make_async_remote_copy(
+            recv_f.at[slot], recv_f.at[slot], sr_sem.at[s], rf_sem.at[slot],
+            device_id=other, device_id_type=MESH_ID,
         )
 
     def start_f(d, c):
         f_copy(d).start()
         return c
 
-    lax.fori_loop(1, n, start_f, 0)
+    lax.fori_loop(1, ns, start_f, 0)
     recv_f[me] = send_f[my_s]
 
     loads[4].wait()
@@ -246,15 +257,21 @@
     for load in loads[5:]:
         load.wait()
 
-    def wait_f(d, c):
-        src = (me + n - d) % n
+    def wait_f(slot):
         pltpu.make_async_remote_copy(
-            send_f.at[0], recv_f.at[src], sf_sem.at[src], rf_sem.at[src],
-            device_id=(src // ns, src % ns), device_id_type=MESH_ID,
+            send_f.at[0], recv_f.at[slot], sf_sem.at[0], rf_sem.at[slot],
+            device_id=other, device_id_type=MESH_ID,
         ).wait_recv()
-        return c
-
-    lax.fori_loop(1, n, wait_f, 0)
+
+    relay(my_s).start()
+
+    def pass_on(d, c):
+        s = ahead(ns - d)
+        wait_f(my_t * ns + s)
+        relay(s).start()
+        return c
+
+    lax.fori_loop(1, ns, pass_on, 0)
 
     group = 8
 
@@ -270,7 +287,15 @@
                 inc[t, :, at] = total
         return c
 
-    lax.fori_loop(0, members // group, add_group, 0)
+    mine, theirs = my_t * (ns // group), (nt - 1 - my_t) * (ns // group)
+    lax.fori_loop(0, ns // group, lambda g, c: add_group(mine + g, c), 0)
+
+    def add_theirs(g, c):
+        for i in range(group):
+            wait_f((theirs + g) * group + i)
+        return add_group(theirs + g, c)
+
+    lax.fori_loop(0, ns // group, add_theirs, 0)
 
     cost_row = back
     for t in range(slots):
@@ -301,46 +326,66 @@
         for j in range(rows):
             upd[t, :, j * LANES : (j + 1) * LANES] = table[t, j * levels : (j + 1) * levels, :]
 
+    def y_copy(d):
+        s = ahead(d)
+        return pltpu.make_async_remote_copy(
+            send_y.at[s], mid_a.at[s], sy_sem.at[s], ry_sem.at[s],
+            device_id=other, device_id_type=MESH_ID,
+        )
+
     def a_copy(d):
-        peer, dev = peer_of(d)
         return pltpu.make_async_remote_copy(
-            send_a.at[peer], recv_a.at[me], sa_sem.at[peer], ra_sem.at[me],
-            device_id=dev, device_id_type=MESH_ID,
+            send_a.at[ahead(d)], recv_a.at[my_s], sa_sem.at[ahead(d)], ra_sem.at[my_s],
+            device_id=(my_t, ahead(d)), device_id_type=MESH_ID,
         )
 
     adj_row[...] = jnp.zeros(adj_row.shape, F32)
 
-    def one_member(d):
-        m = (me + d) % n
+    def one_member(m):
         for j in range(rows):
             at = pl.ds(j * LANES, LANES)
             z = sum(perturb[t, m, :, at].astype(F32) * upd[t, :, at] for t in range(slots))
             adj_row[j : j + 1, :] = jnp.sum(z, axis=0, keepdims=True)
-        send_a[m] = adj_row[...].astype(BF16)
-
-    one_member(1)
-
-    def next_member(d, c):
-        one_member(d)
+
+    def to_other(d):
+        one_member((nt - 1 - my_t) * ns + ahead(d))
+        send_y[ahead(d)] = adj_row[...].astype(BF16)
+
+    def next_other(d, c):
+        to_other(d)
+        y_copy(d - 1).start()
+        return c
+
+    def to_owner(d):
+        s = ahead(d)
+        one_member(my_t * ns + s)
+        y_copy(d).wait_recv()
+        send_a[s] = (adj_row[...] + mid_a[s].astype(F32)).astype(BF16)
+
+    def next_owner(d, c):
+        to_owner(d)
         a_copy(d - 1).start()
         return c
 
-    lax.fori_loop(2, n + 1, next_member, 0)
-    recv_a[me] = send_a[me]
+    to_other(1)
+    lax.fori_loop(2, ns + 1, next_other, 0)
+    y_copy(ns).start()
+    to_owner(1)
+    lax.fori_loop(2, ns + 1, next_owner, 0)
+    recv_a[my_s] = send_a[my_s]
 
     def wait_a(d, c):
-        src = (me + n - d) % n
+        src = ahead(ns - d)
         pltpu.make_async_remote_copy(
             send_a.at[0], recv_a.at[src], sa_sem.at[src], ra_sem.at[src],
-            device_id=(src // ns, src % ns), device_id_type=MESH_ID,
+            device_id=(my_t, src), device_id_type=MESH_ID,
         ).wait_recv()
         return c
 
-    lax.fori_loop(1, n, wait_a, 0)
+    lax.fori_loop(1, ns, wait_a, 0)
 
     for s in range(ns):
-        whole = sum(recv_a[t * ns + s].astype(F32) for t in range(nt))
-        flat[s * rows : (s + 1) * rows, :] = whole[:rows]
+        flat[s * rows : (s + 1) * rows, :] = recv_a[s].astype(F32)[:rows]
     mid = dot_left(cxp, unfold(wide_of(flat)))
     gr = ctl + spec * fold(dot_right(mid, cyt))
     grad[...] = gr
@@ -368,13 +413,20 @@
         a_copy(d).wait_send()
         return c
 
-    lax.fori_loop(1, n, drain, 0)
+    lax.fori_loop(1, ns, drain, 0)
+
+    def drain_y(d, c):
+        relay(ahead(d)).wait_send()
+        y_copy(d).wait_send()
+        return c
+
+    lax.fori_loop(1, ns + 1, drain_y, 0)
 
     def wait_s(d, c):
-        src = (me + n - d) % n
+        src = lax.rem(me + n - d, n)
         pltpu.make_async_remote_copy(
             part, parts.at[src], sp_sem.at[src], rp_sem.at[src],
-            device_id=(src // ns, src % ns), device_id_type=MESH_ID,
+            device_id=(lax.div(src, ns), lax.rem(src, ns)), device_id_type=MESH_ID,
         ).wait_recv()
         return c
 
@@ -429,12 +481,11 @@
             pltpu.VMEM((slots, LANES, obs), BF16),
             pltpu.VMEM((slots, levels, piece), F32),
             pltpu.VMEM((pad_rows, LANES), F32),
-            pltpu.VMEM((n, pad_rows, LANES), BF16),
-            pltpu.VMEM((n, pad_rows, LANES), BF16),
+            *[pltpu.VMEM((ns, pad_rows, LANES), BF16)] * 4,
             pltpu.VMEM((2, LANES), F32),
             pltpu.VMEM((n, 2, LANES), F32),
             pltpu.VMEM((GX // FOLD, FOLD * GY), F32),
-            dma((n,)), dma((n,)), dma((n,)), dma((n,)), dma((n,)), dma((n,)),
+            dma((ns,)), dma((n,)), *[dma((ns,))] * 5, dma((n,)), dma((n,)),
         ],
         compiler_params=pltpu.CompilerParams(
             collective_id=0, has_side_effects=True, vmem_limit_bytes=67043328
@@ -448,11 +499,12 @@
     n = nt * ns
     piece = GX * GY // ns
     return (
-        control.shape[0] == n
+        nt == 2
+        and ns % 8 == 0
+        and control.shape[0] == n
         and piece % LANES == 0
         and (FOLD * GY) % LANES == 0
         and (GX // FOLD) % 8 == 0
-        and n % 8 == 0
         and (innovation.shape[1] // ns) % LANES == 0
     )
 

time: 38.6 us -> 38.3 us (level)
  no operation moved by 1% of the time
where the time goes in v3:
time: 38.3 us; the launch traced here: 38.1 us
  Pallas kernels  34.2 us (89%)
  between operations  2.33 us (6%)
  local copies, waits for them, and re-layouts  1.62 us (4%)
    pallas_call x1, Pallas kernels, fused_device(): pl.pallas_call(functools.partial(step_kernel, nt, ns, len(sources)), out_...  34.2 us
    unnamed x1, local copies, waits for them, and re-layouts  1.62 us

profile of v3, /device:TPU:0, one launch (start us, length us, event | category | flops | bytes accessed | tf_op | source)
XLA Modules:
  0.0 38.1 jit_solution(7588249489710537458)
XLA Ops:
  0.6 34.2 %envar_step.1 = (f32[400,128]{1,0:T(8,128)}, f32[1,128]{1,0:T(1,128)}) custom-call(f32[400,128]{1,0:T(8,128)} %bitcast.6, f32[400,128]{1,0:T(8,128)} %bitcast.7, bf16[2,160,160]{2,1,0:T(8,128)(2,1)} %constant.10.clone.refs_2_, bf16[2,320,320]{2,1,0:T(8,128)(2,1)} %constant.9.clone.refs_3_, s32[2,2048]{1,0:T(2,128)} %refs_4_.1, ...), custom_call_target="tpu_custom_call" | custom-call | tf_op jit(solution)/shard_map/envar_step/pallas_call | solution.py:464
  34.8 1.6 %copy.15 = f32[1,51200]{1,0:T(1,128)} copy(f32[1,51200]{1,0:T(1,128)} %bitcast.5) | data formatting | bytes 409600
